TPU v7x, 32 devices: a whole 2x2x4 slice. The times are simulated.
32 devices in a mesh: head: 4 (over y, x), ctx: 8 (over z, core).
Axes of the slice: x: 2, y: 2, z: 4, core: 2. Of those that a mesh axis runs over, the one named last changes fastest.
Arguments:
- mla_queries: bfloat16 [128, 128, 576], P('head'), may hold values from -4 to 4
- latent_cache: bfloat16 [32768, 576], P('ctx'), may hold values from -4 to 4
- normalizers: float32 [128, 128], P('head'), may hold values from 9 to 15
- query_positions: int32 [128], replicated, may hold values from 0 to 65535, as said below
- key_positions: int32 [32768], P('ctx'), may hold values from 0 to 65535, as said below
- index_queries: bfloat16 [64, 128, 128], P('head'), may hold values from -24 to 24
- index_keys: bfloat16 [32768, 128], P(('ctx', 'head')), may hold values from -24 to 24
- index_weights: bfloat16 [64, 128], P('head'), may hold values from -16 to 16
Outputs:
- grad_queries: float32 [64, 128, 128], P('head')
- grad_weights: float32 [64, 128], P('head')
- grad_keys: float32 [32768, 128], P(('ctx', 'head'))
Inputs may be any that keep to these rules, and one draw needn't show every extreme that they name: `query_positions`: every query position is one the keys' positions could reach. `key_positions`: key positions rise strictly along the keys.
All inputs are finite; a program needn't handle non-finite values.
Results may differ from a plain program's by a relative error of at most 0.00115.
The roundings to bfloat16 on the way count: a program that leaves them out, or rounds other values in their place, can miss the bound.
Values may be sent and summed in bfloat16 or wider, within the bound.
A program may use at most 128 MiB of HBM per device.

v0:
```python
import math

import jax
import jax.numpy as jnp
from jax import lax
from jax.sharding import PartitionSpec as P

att_scale = 192.0 ** (-0.5)
loss_scale = 1024.0
masked_floor = -1e30


def per_device(
    mla_queries,
    latent_cache,
    normalizers,
    query_positions,
    key_positions,
    index_queries,
    index_keys,
    index_weights,
):
    head_count = mla_queries.shape[0]
    query_count = mla_queries.shape[1]
    query_flat = mla_queries.reshape(head_count * query_count, mla_queries.shape[2])
    sub_keys = index_keys.shape[0]
    block_rows = math.gcd(sub_keys * lax.axis_size("head"), 512)

    def one_block(block_index):
        first_row = block_index * block_rows
        cache_rows = lax.dynamic_slice_in_dim(latent_cache, first_row, block_rows, 0)
        positions = lax.dynamic_slice_in_dim(key_positions, first_row, block_rows, 0)
        scores = jnp.dot(cache_rows, query_flat.T, preferred_element_type=jnp.float32)
        scores = scores.reshape(block_rows, head_count, query_count)
        weights = jnp.exp(scores * att_scale - normalizers[None])
        visible = positions[:, None] <= query_positions[None, :]
        return jnp.where(visible, jnp.sum(weights, axis=1), 0.0)

    pieces = lax.map(
        one_block, jnp.arange(sub_keys * lax.axis_size("head") // block_rows, dtype=jnp.int32)
    )
    summed_probs = lax.psum_scatter(
        pieces.reshape(sub_keys * lax.axis_size("head"), query_count),
        "head",
        scatter_dimension=0,
        tiled=True,
    )
    all_queries, all_weights = (
        lax.all_gather(index_queries, "head", axis=0, tiled=True),
        lax.all_gather(index_weights, "head", axis=0, tiled=True),
    )
    index_heads = all_queries.shape[0]
    index_width = all_queries.shape[2]
    offset = lax.axis_index("head") * sub_keys
    own_positions = lax.dynamic_slice_in_dim(key_positions, offset, sub_keys, 0)
    visible = own_positions[:, None] <= query_positions[None, :]
    pair_flat = all_queries.reshape(index_heads * query_count, index_width)
    relu_input = jnp.dot(index_keys, pair_flat.T, preferred_element_type=jnp.float32)
    relu_input = relu_input.reshape(sub_keys, index_heads, query_count)
    index_scale = (index_heads * index_width) ** (-0.5)
    activated = jnp.maximum(relu_input, 0.0)
    weights_float = all_weights.astype(jnp.float32)
    logits = index_scale * jnp.sum(activated * weights_float[None], axis=1)
    hidden_logits = jnp.where(visible, logits, masked_floor)
    local_max = jnp.max(hidden_logits, axis=0)
    local_target = jnp.sum(summed_probs, axis=0)
    row_max = lax.pmax(local_max, ("head", "ctx"))
    local_exp = jnp.sum(jnp.where(visible, jnp.exp(hidden_logits - row_max[None]), 0.0), axis=0)
    row_total, target_total = lax.psum((local_exp, local_target), ("head", "ctx"))
    softmax_probs = (
        jnp.where(visible, jnp.exp(hidden_logits - row_max[None]), 0.0) / row_total[None]
    )
    target = summed_probs / target_total[None]
    logit_grad = loss_scale * jnp.where(visible, softmax_probs - target, 0.0)
    gradient_gate = jnp.where(relu_input > 0.0, index_scale * weights_float[None], 0.0)
    pre_grad = (gradient_gate * logit_grad[:, None, :]).astype(jnp.bfloat16)
    pre_flat = pre_grad.reshape(sub_keys, index_heads * query_count)
    grad_weights_part = index_scale * jnp.sum(activated * logit_grad[:, None, :], axis=0)
    grad_queries_part = jnp.dot(pre_flat.T, index_keys, preferred_element_type=jnp.float32)
    grad_queries_part = grad_queries_part.reshape(index_heads, query_count, index_width)
    grad_keys = jnp.dot(pre_flat, pair_flat, preferred_element_type=jnp.float32)
    head_queries, head_weights = (
        lax.psum_scatter(grad_queries_part, "head", scatter_dimension=0, tiled=True),
        lax.psum_scatter(grad_weights_part, "head", scatter_dimension=0, tiled=True),
    )
    grad_queries, grad_weights = lax.psum((head_queries, head_weights), "ctx")
    return (grad_queries, grad_weights, grad_keys)


def solution(mesh):
    placed = (
        P("head", None, None),
        P("ctx", None),
        P("head", None),
        P(),
        P("ctx"),
        P("head", None, None),
        P(("ctx", "head"), None),
        P("head", None),
    )
    return jax.shard_map(
        per_device,
        mesh=mesh,
        in_specs=placed,
        out_specs=(P("head", None, None), P("head", None), P(("ctx", "head"), None)),
        check_vma=False,
    )
```

profile of v0, /device:TPU:1, one launch (start us, length us, event | category | flops | bytes accessed | tf_op | source)
XLA Modules:
  0.0 361.6 jit_solution(2272347219969455144)
XLA Ops:
  8.0 7.7 %copy.14 = bf16[32,128,576]{2,1,0:T(8,128)(2,1)} copy(bf16[32,128,576]{1,2,0:T(8,128)(2,1)} %param.10) | data formatting | bytes 9437184 | tf_op args[0]
  15.7 98.6 %while.10 = (s32[]{:T(128)}, f32[8,512,128]{2,1,0:T(8,128)S(1)}, s32[8]{0:T(128)S(1)}, s32[4096]{0:T(1024)}, s32[128]{0:T(128)S(1)}, /*index=5*/bf16[4096,576]{0...) while((s32[]{:T(128)}, f32[8,512,128]{2,1,0:T(8,128)S(1)}, ...), condition=%wide.region_7.8_spmd, body=%wide.region_5.7_spmd.sunk | while | flops 2422276096 | bytes 40196800 | solution.py:39
  17.7 5.8 %multiply_bitcast_fusion.2 = f32[64,8,32,128]{3,1,2,0:T(8,128)S(1)} fusion(bf16[4096,576]{1,0:T(8,128)(2,1)} %get-tuple-element.145, bf16[4096,576]{0,1:T(8,128)(2,1)} %get-tuple-element.144, s32[]{:T(128)S(6)} %select_n.68), kind=kOutput, calls=%fused_computation.3.clone.1 | convolution fusion | flops 2418016256 | bytes 14221316 | tf_op jit(solution)/shard_map/while/body/eval_jaxpr/dot_general | solution.py:33
  25.3 2.7 fusion.26
  30.2 5.6 %multiply_bitcast_fusion.2 = f32[64,8,32,128]{3,1,2,0:T(8,128)S(1)} fusion(bf16[4096,576]{1,0:T(8,128)(2,1)} %get-tuple-element.145, bf16[4096,576]{0,1:T(8,128)(2,1)} %get-tuple-element.144, s32[]{:T(128)S(6)} %select_n.68), kind=kOutput, calls=%fused_computation.3.clone.1 | convolution fusion | flops 2418016256 | bytes 14221316 | tf_op jit(solution)/shard_map/while/body/eval_jaxpr/dot_general | solution.py:33
  37.6 2.7 fusion.26
  42.5 5.6 %multiply_bitcast_fusion.2 = f32[64,8,32,128]{3,1,2,0:T(8,128)S(1)} fusion(bf16[4096,576]{1,0:T(8,128)(2,1)} %get-tuple-element.145, bf16[4096,576]{0,1:T(8,128)(2,1)} %get-tuple-element.144, s32[]{:T(128)S(6)} %select_n.68), kind=kOutput, calls=%fused_computation.3.clone.1 | convolution fusion | flops 2418016256 | bytes 14221316 | tf_op jit(solution)/shard_map/while/body/eval_jaxpr/dot_general | solution.py:33
  49.9 2.7 fusion.26
  54.8 5.6 %multiply_bitcast_fusion.2 = f32[64,8,32,128]{3,1,2,0:T(8,128)S(1)} fusion(bf16[4096,576]{1,0:T(8,128)(2,1)} %get-tuple-element.145, bf16[4096,576]{0,1:T(8,128)(2,1)} %get-tuple-element.144, s32[]{:T(128)S(6)} %select_n.68), kind=kOutput, calls=%fused_computation.3.clone.1 | convolution fusion | flops 2418016256 | bytes 14221316 | tf_op jit(solution)/shard_map/while/body/eval_jaxpr/dot_general | solution.py:33
  67.1 5.6 %multiply_bitcast_fusion.2 = f32[64,8,32,128]{3,1,2,0:T(8,128)S(1)} fusion(bf16[4096,576]{1,0:T(8,128)(2,1)} %get-tuple-element.145, bf16[4096,576]{0,1:T(8,128)(2,1)} %get-tuple-element.144, s32[]{:T(128)S(6)} %select_n.68), kind=kOutput, calls=%fused_computation.3.clone.1 | convolution fusion | flops 2418016256 | bytes 14221316 | tf_op jit(solution)/shard_map/while/body/eval_jaxpr/dot_general | solution.py:33
  79.4 5.6 %multiply_bitcast_fusion.2 = f32[64,8,32,128]{3,1,2,0:T(8,128)S(1)} fusion(bf16[4096,576]{1,0:T(8,128)(2,1)} %get-tuple-element.145, bf16[4096,576]{0,1:T(8,128)(2,1)} %get-tuple-element.144, s32[]{:T(128)S(6)} %select_n.68), kind=kOutput, calls=%fused_computation.3.clone.1 | convolution fusion | flops 2418016256 | bytes 14221316 | tf_op jit(solution)/shard_map/while/body/eval_jaxpr/dot_general | solution.py:33
  91.7 5.6 %multiply_bitcast_fusion.2 = f32[64,8,32,128]{3,1,2,0:T(8,128)S(1)} fusion(bf16[4096,576]{1,0:T(8,128)(2,1)} %get-tuple-element.145, bf16[4096,576]{0,1:T(8,128)(2,1)} %get-tuple-element.144, s32[]{:T(128)S(6)} %select_n.68), kind=kOutput, calls=%fused_computation.3.clone.1 | convolution fusion | flops 2418016256 | bytes 14221316 | tf_op jit(solution)/shard_map/while/body/eval_jaxpr/dot_general | solution.py:33
  104.0 5.6 %multiply_bitcast_fusion.2 = f32[64,8,32,128]{3,1,2,0:T(8,128)S(1)} fusion(bf16[4096,576]{1,0:T(8,128)(2,1)} %get-tuple-element.145, bf16[4096,576]{0,1:T(8,128)(2,1)} %get-tuple-element.144, s32[]{:T(128)S(6)} %select_n.68), kind=kOutput, calls=%fused_computation.3.clone.1 | convolution fusion | flops 2418016256 | bytes 14221316 | tf_op jit(solution)/shard_map/while/body/eval_jaxpr/dot_general | solution.py:33
  116.9 7.0 %all_gather.7 = bf16[64,128]{1,0:T(8,128)(2,1)S(1)} all-gather(bf16[16,128]{1,0:T(8,128)(2,1)S(1)} %copy-done.4), channel_id=1, replica_groups=mesh['head'=4,'ctx'=8] {'head'}, dimensions={0}, use_global_device_ids=true | all-gather | bytes 20480 | tf_op jit(solution)/shard_map/all_gather | solution.py:50
  124.0 15.0 %multiply_reduce_fusion.1 = (f32[1024,128]{0,1:T(8,128)S(1)}, f32[1024,64,128]{0,2,1:T(8,128)}) fusion(f32[64,128]{1,0:T(8,128)S(1)} %convert_element_type.6, bf16[64,128,128]{2,1,0:T(8,128)(2,1)} %all-gather.2.cloned.1.call-done, bf16[1024,128]{1,0:T(8,128)(2,1)S(1)} %copy-done), kind=kOutput, calls=%fused_computation.10 | convolution fusion | flops 2172518400 | bytes 36470784 | tf_op jit(solution)/shard_map/dot_general | solution.py:58
  139.2 40.9 %pmax.7 = f32[128]{0:T(128)S(1)} all-reduce(f32[128]{0:T(128)S(1)} %fusion.10), channel_id=1, replica_groups=mesh['head'=4,'ctx'=8] {'head','ctx'}, use_global_device_ids=true, to_apply=%region_2.3 | all-reduce | flops 128 | bytes 1024 | tf_op jit(solution)/shard_map/pmax | solution.py:67
  181.6 41.1 %all-reduce.1 = (f32[128]{0:T(128)S(1)}, f32[128]{0:T(128)S(1)}) all-reduce(f32[128]{0:T(128)S(1)} %reduce_sum.49, f32[128]{0:T(128)S(1)} %fusion.11), channel_id=1, replica_groups=mesh['head'=4,'ctx'=8] {'head','ctx'}, use_global_device_ids=true, to_apply=%region_10.11 | all-reduce | flops 256 | bytes 2048 | tf_op jit(solution)/shard_map/psum | solution.py:69
  224.0 15.7 %fusion.5 = f32[64,128,128]{2,1,0:T(8,128)} fusion(f32[1024,64,128]{0,2,1:T(8,128)} %get-tuple-element.65, f32[1024,128]{0,1:T(8,128)S(1)} %fusion.9, f32[64,128]{1,0:T(8,128)S(1)} %broadcast_multiply_fusion.1, bf16[1024,128]{1,0:T(8,128)(2,1)S(1)} %copy-done), kind=kOutput, calls=%fused_computation.11 | convolution fusion | flops 2181038080 | bytes 38567936 | tf_op jit(solution)/shard_map/dot_general | solution.py:79
  241.0 14.3 %fusion.8 = f32[1024,128]{1,0:T(8,128)} fusion(bf16[64,128,128]{2,1,0:T(8,128)(2,1)S(1)} %copy-done.1, f32[1024,64,128]{0,2,1:T(8,128)} %get-tuple-element.65, f32[1024,128]{0,1:T(8,128)S(1)} %fusion.9, f32[64,128]{1,0:T(8,128)S(1)} %broadcast_multiply_fusion.1), kind=kOutput, calls=%fused_computation.14 | convolution fusion | flops 2181038080 | bytes 36732928 | tf_op jit(solution)/shard_map/dot_general | solution.py:81
  255.4 37.5 %reduce-scatter.5.cloned.1.call-done = f32[16,128,128]{2,1,0:T(8,128)} async-done(((f32[64,128,128]{2,1,0:T(8,128)}), f32[16,128,128]{2,1,0:T(8,128)}) %reduce-scatter.5.cloned.1.call-update) | async-done | bytes 1048592 | tf_op jit(solution)/shard_map/reduce_scatter | solution.py:83
  292.9 15.4 %multiply_reduce_fusion = f32[64,128]{1,0:T(8,128)S(1)} fusion(f32[1024,64,128]{0,2,1:T(8,128)} %get-tuple-element.65, f32[1024,128]{0,1:T(8,128)S(1)} %fusion.9), kind=kLoop, calls=%fused_computation.8 | loop fusion | flops 25157632 | bytes 34111488 | tf_op jit(solution)/shard_map/reduce_sum | solution.py:78
  308.3 12.0 %all-reduce = f32[64,128]{1,0:T(8,128)S(1)} all-reduce(f32[64,128]{1,0:T(8,128)S(1)} %broadcast_multiply_fusion), channel_id=4, replica_groups=mesh['head'=4,'ctx'=8] {'head'}, use_global_device_ids=true, to_apply=%region_14.15.clone | all-reduce | flops 8192 | bytes 65536
  320.3 18.1 %psum.31 = f32[16,128]{1,0:T(8,128)} all-reduce(f32[16,128]{1,0:T(8,128)S(1)} %constant_dynamic-slice_fusion), channel_id=1, replica_groups=mesh['head'=4,'ctx'=8] {'ctx'}, use_global_device_ids=true, to_apply=%region_15.16 | all-reduce | flops 2048 | bytes 16384 | tf_op jit(solution)/shard_map/psum | solution.py:86
  338.5 14.3 %all-reduce.4.cloned.1.call-done = f32[16,128,128]{2,1,0:T(8,128)} async-done(((f32[16,128,128]{2,1,0:T(8,128)}), f32[16,128,128]{2,1,0:T(8,128)}) %all-reduce.4.cloned.1.call-update) | async-done | bytes 1048592 | tf_op jit(solution)/shard_map/psum | solution.py:86
  (73 shorter events, 49.2 us)
Async XLA Ops:
  7.2 116.8 %copy-start = (bf16[1024,128]{1,0:T(8,128)(2,1)S(1)}, bf16[1024,128]{1,0:T(8,128)(2,1)}, u32[]{:S(2)}) copy-start(bf16[1024,128]{1,0:T(8,128)(2,1)} %param.16) | copy-start | bytes 786436
  7.2 8.5 %copy-start.3 = (s32[128]{0:T(128)S(1)}, s32[128]{0:T(128)}, u32[]{:S(2)}) copy-start(s32[128]{0:T(128)} %param.13) | copy-start | bytes 1540
  7.2 8.5 %copy-start.2 = (f32[32,128]{1,0:T(8,128)S(1)}, f32[32,128]{1,0:T(8,128)}, u32[]{:S(2)}) copy-start(f32[32,128]{1,0:T(8,128)} %param.12) | copy-start | bytes 49156
  7.2 116.8 %all-gather.2.cloned.1.call-start = ((), (), s32[]{:S(2)}) async-start(), calls=%async_computation.2 | async-start | bytes 2621440 | tf_op jit(solution)/shard_map/all_gather | solution.py:49
  7.9 172.5 %reduce-scatter.3.cloned.1.call-start = ((), (), s32[]{:S(2)}) async-start(), calls=%async_computation.3 | async-start | bytes 2621440 | tf_op jit(solution)/shard_map/reduce_scatter | solution.py:42
  15.7 101.2 %copy-start.4 = (bf16[16,128]{1,0:T(8,128)(2,1)S(1)}, bf16[16,128]{1,0:T(8,128)(2,1)}, u32[]{:S(2)}) copy-start(bf16[16,128]{1,0:T(8,128)(2,1)} %param.17) | copy-start | bytes 12292
  116.1 176.8 %reduce-scatter.5.cloned.1.call-start = ((), (), s32[]{:S(2)}) async-start(), calls=%async_computation.4 | async-start | bytes 5242880 | tf_op jit(solution)/shard_map/reduce_scatter | solution.py:83
  224.0 15.8 %copy-start.5 = (u32[32]{0:T(128)S(1)}, u32[32]{0:T(128)}, u32[]{:S(2)}) copy-start(u32[32]{0:T(128)} %constant.44) | copy-start | bytes 388
  224.0 17.0 %copy-start.1 = (bf16[64,128,128]{2,1,0:T(8,128)(2,1)S(1)}, bf16[64,128,128]{2,1,0:T(8,128)(2,1)}, u32[]{:S(2)}) copy-start(bf16[64,128,128]{2,1,0:T(8,128)(2,1)} %all-gather.2.cloned.1.call-done) | copy-start | bytes 6291460
  239.7 113.1 %all-reduce.4.cloned.1.call-start = ((), (), s32[]{:S(2)}) async-start(), calls=%async_computation.5 | async-start | bytes 2097152 | tf_op jit(solution)/shard_map/psum | solution.py:86
Sparse Core Ops, SparseCore 0:
  9.9 37.0 all-gather.1
  116.3 37.6 reduce-scatter.2
  239.8 53.0 reduce-scatter.4
  295.1 57.6 all-reduce.3
where the time goes:
time: 365 us; the launch traced here: 362 us
  blocking collectives  119 us (33%)
  matrix products  90.2 us (25%)
  waiting for transfers between devices  52.6 us (14%)
  other arithmetic  40.7 us (11%)
  local copies, waits for them, and re-layouts  38.5 us (11%)
  between operations  14.6 us (4%)
  loops' own time  5.59 us (2%)
    dot_general x8, matrix products, one_block(): jnp.dot(cache_rows, query_flat.T, preferred_element_type=jnp.float32)  45.2 us
    psum x1, blocking collectives, per_device(): lax.psum((local_exp, local_target), ('head', 'ctx'))  41.1 us
    pmax x1, blocking collectives, per_device(): row_max = lax.pmax(local_max, ('head', 'ctx'))  40.9 us
    reduce_scatter x1, waiting for transfers between devices, per_device(): lax.psum_scatter(grad_queries_part, 'head', scatter_dimension=0, tiled=True)  37.5 us
    reduce_sum x8, other arithmetic, one_block(): return jnp.where(visible, jnp.sum(weights, axis=1), 0.0)  21.3 us
    psum x1, blocking collectives, per_device(): grad_queries, grad_weights = lax.psum((head_queries, head_weights), 'ctx')  18.1 us
    dot_general x1, matrix products, per_device(): jnp.dot(pre_flat.T, index_keys, preferred_element_type=jnp.float32)  15.7 us
    reduce_sum x1, other arithmetic, per_device(): jnp.sum(activated * logit_grad[:, None, :], axis=0)  15.4 us
  transfers between devices with their start and end apart: 4, of which 2 were waited for; matrix products, arithmetic and copies ran while one was open for 41% of the time, Pallas kernels for 0%

commit v1 on v0

v1 whole, which is shorter than its diff:
```python
import functools
import math

import jax
import jax.numpy as jnp
from jax import lax
from jax.experimental import pallas as pl
from jax.experimental.pallas import tpu as pltpu
from jax.sharding import PartitionSpec as P

att_scale = 192.0 ** (-0.5)
loss_scale = 1024.0
masked_floor = -1e30
log2e = 1.4426950408889634
MESH = pl.DeviceIdType.MESH
NT = (((1,), (1,)), ((), ()))
NN = (((1,), (0,)), ((), ()))


def dot(a, b, dims):
    return lax.dot_general(a, b, dims, preferred_element_type=jnp.float32)


def kernel(
    q_ref, cache_ref, norm_ref, qpos_ref, kpos_ref, iq_ref, keys_ref, iw_ref,
    res_ref, gk_ref,
    part, rp, qs, ws, keys_t, lg, stat, stat_h, stat2, stat_c, pre,
    gbuf, pr, hs, hr, cs, zr, fin, res, nrm,
    s_part, r_part, s_q, r_q, s_w, r_w, s_sh, r_sh, s_sc, r_sc,
    s_pair, r_pair, s_head, r_head, s_z, r_z, s_ag, r_ag, s_fw, r_fw,
):
    n = lax.axis_size("head")
    nc = lax.axis_size("ctx")
    nz = nc // 2
    me = lax.axis_index("head")
    mc = lax.axis_index("ctx")
    par = lax.rem(mc, 2)
    z = lax.div(mc, 2)
    partner = z * 2 + (1 - par)
    sub, width = keys_ref.shape
    qn = qpos_ref.shape[1]
    hl = iw_ref.shape[0]
    mh = q_ref.shape[0] // qn
    nch = hl // nz
    nstep = nch * n
    iscale = (n * hl * width) ** (-0.5)

    def to_head(r):
        return {"head": lax.rem(me + r, n)}

    def head_copy(src, dst, ss, rs, r):
        return pltpu.make_async_remote_copy(
            src_ref=src, dst_ref=dst, send_sem=ss, recv_sem=rs,
            device_id=to_head(r), device_id_type=MESH)

    def ctx_copy(src, dst, ss, rs, c):
        return pltpu.make_async_remote_copy(
            src_ref=src, dst_ref=dst, send_sem=ss, recv_sem=rs,
            device_id={"ctx": c}, device_id_type=MESH)

    ws[0] = iw_ref[...].astype(jnp.float32)
    barrier = pltpu.get_barrier_semaphore()
    for r in range(1, n):
        pl.semaphore_signal(barrier, inc=1, device_id=to_head(r), device_id_type=MESH)
    for r in range(1, nc):
        pl.semaphore_signal(
            barrier, inc=1, device_id={"ctx": lax.rem(mc + r, nc)}, device_id_type=MESH)
    keys_t[...] = keys_ref[...].T
    qs[0] = iq_ref[...]
    nrm[...] = norm_ref[...] * log2e
    pl.semaphore_wait(barrier, n - 1 + nc - 1)

    q_copies = []
    for r in range(1, n):
        q_copies.append(head_copy(iq_ref, qs.at[r], s_q.at[r - 1], r_q.at[r - 1], r))
        q_copies.append(head_copy(ws.at[0], ws.at[r], s_w.at[r - 1], r_w.at[r - 1], r))
    for copy in q_copies:
        copy.start()

    rows = min(sub, 512)
    nblk = sub // rows
    hg = 4

    def part_copy(r, b):
        span = pl.ds(pl.multiple_of(b * rows, rows), rows)
        return head_copy(
            part.at[r, span], rp.at[r - 1, span],
            s_part.at[(r - 1) * nblk + b], r_part.at[(r - 1) * nblk + b], r)

    def mla_step(i, carry):
        r = lax.rem(lax.div(i, nblk) + 1, n)
        b = lax.rem(i, nblk)
        first = lax.rem(me + r, n) * sub + b * rows
        cache = cache_ref[pl.ds(pl.multiple_of(first, rows), rows), :]
        span = pl.ds(pl.multiple_of(b * rows, rows), rows)

        def group(g, acc_unused):
            qg = q_ref[pl.ds(pl.multiple_of(g * (hg * qn), hg * qn), hg * qn), :]
            x = dot(cache, qg, NT)
            total = None
            for h in range(hg):
                e = jnp.exp2(
                    x[:, h * qn:(h + 1) * qn] * (att_scale * log2e)
                    - nrm[pl.ds(g * hg + h, 1), :])
                total = e if total is None else total + e

            @pl.when(g == 0)
            def _():
                part[r, span, :] = total

            @pl.when(g > 0)
            def _():
                part[r, span, :] = part[r, span, :] + total

            return acc_unused

        lax.fori_loop(0, mh // hg, group, 0)

        @pl.when(r > 0)
        def _():
            part_copy(r, b).start()

        return carry

    lax.fori_loop(0, n * nblk, mla_step, 0)

    for copy in q_copies:
        copy.wait()
    lg[...] = jnp.zeros_like(lg)
    srows = min(sub, 256)
    ih = nz

    def logit_step(i, carry):
        r = lax.div(i, hl // ih)
        k = lax.rem(i, hl // ih)
        qg = qs[r, pl.ds(pl.multiple_of(k * (ih * qn), ih * qn), ih * qn), :]
        wg = ws[r, pl.ds(k * ih, ih), :]
        for sb in range(sub // srows):
            span = slice(sb * srows, (sb + 1) * srows)
            x = dot(keys_ref[span, :], qg, NT)
            total = lg[span, :]
            for h in range(ih):
                total = total + jnp.maximum(x[:, h * qn:(h + 1) * qn], 0.0) * wg[h:h + 1, :]
            lg[span, :] = total
        return carry

    lax.fori_loop(0, n * (hl // ih), logit_step, 0)

    for r in range(1, n):
        for b in range(nblk):
            part_copy(r, b).wait()
    visible = kpos_ref[...] <= qpos_ref[...]
    probs = part[0]
    for r in range(1, n):
        probs = probs + rp[r - 1]
    probs = jnp.where(visible, probs, 0.0)
    part[0] = probs
    hidden = jnp.where(visible, lg[...] * iscale, masked_floor)
    lg[...] = hidden
    local_max = jnp.max(hidden, axis=0, keepdims=True)
    local_sum = jnp.sum(
        jnp.where(visible, jnp.exp(hidden - local_max), 0.0), axis=0, keepdims=True)
    local_target = jnp.sum(probs, axis=0, keepdims=True)

    def exchange(own, mine, theirs, count, copy_of):
        mine[0:1, :] = own[0]
        mine[1:2, :] = own[1]
        mine[2:3, :] = own[2]
        mine[3:8, :] = jnp.zeros_like(mine[3:8, :])
        copies = [copy_of(r) for r in range(1, count)]
        for copy in copies:
            copy.start()
        for copy in copies:
            copy.wait()
        top = own[0]
        for r in range(1, count):
            top = jnp.maximum(top, theirs[r - 1, 0:1, :])
        total = own[1] * jnp.exp(own[0] - top)
        goal = own[2]
        for r in range(1, count):
            total = total + theirs[r - 1, 1:2, :] * jnp.exp(theirs[r - 1, 0:1, :] - top)
            goal = goal + theirs[r - 1, 2:3, :]
        return top, total, goal

    stats = exchange(
        (local_max, local_sum, local_target), stat, stat_h, n,
        lambda r: head_copy(stat, stat_h.at[r - 1], s_sh.at[r - 1], r_sh.at[r - 1], r))
    stats = exchange(
        stats, stat2, stat_c, nc,
        lambda r: ctx_copy(
            stat2, stat_c.at[r - 1], s_sc.at[r - 1], r_sc.at[r - 1], lax.rem(mc + r, nc)))
    row_max, row_total, target_total = stats
    soft = jnp.exp(lg[...] - row_max) * (1.0 / row_total)
    lg[...] = loss_scale * jnp.where(visible, soft - part[0] * (1.0 / target_total), 0.0)
    gk_ref[...] = jnp.zeros_like(gk_ref)

    half = width // 2
    tail = gbuf.shape[3] - half

    def pair_copy(i):
        return ctx_copy(gbuf.at[i, 1 - par], pr.at[i], s_pair.at[i], r_pair.at[i], partner)

    def head_send(i, k, r):
        return head_copy(hs.at[i], hr.at[k, r - 1], s_head.at[i], r_head.at[k * n + r], n - r)

    def z_copy(k, d):
        to = lax.rem(z + d, nz)
        at = k * nz + d
        return ctx_copy(cs.at[k, to], zr.at[k, d - 1], s_z.at[at], r_z.at[at], to * 2 + par)

    def ag_copy(k, d):
        to = lax.rem(z + d, nz)
        at = k * nz + d
        return ctx_copy(fin.at[k], res.at[0, k, d - 1], s_ag.at[at], r_ag.at[at], to * 2 + par)

    def fw_copy(k, d):
        at = k * nz + d
        src = fin.at[k] if d == 0 else res.at[0, k, d - 1]
        dst = res.at[1, k, nz - 1 if d == 0 else d - 1]
        return ctx_copy(src, dst, s_fw.at[at], r_fw.at[at], partner)

    def stage_pair(i):
        pair_copy(i).wait_recv()
        hs[i] = gbuf[i, par] + pr[i]
        k = lax.div(i, n)
        r = lax.rem(lax.rem(i, n) + 1, n)

        @pl.when(r > 0)
        def _():
            head_send(i, k, r).start()

    def stage_head(k):
        total = hs[k * n + n - 1]
        for r in range(1, n):
            head_send(k * n + r - 1, k, r).wait_recv()
            total = total + hr[k, r - 1]
        cs[k] = total
        for d in range(1, nz):
            z_copy(k, d).start()

    def stage_z(k):
        total = cs[k, z]
        for d in range(1, nz):
            z_copy(k, d).wait_recv()
            total = total + zr[k, d - 1]
        fin[k] = total
        for d in range(1, nz):
            ag_copy(k, d).start()
        fw_copy(k, 0).start()

    def stage_ag(k):
        for d in range(1, nz):
            ag_copy(k, d).wait_recv()
            fw_copy(k, d).start()

    def grad_step(i, carry):
        k = lax.div(i, n)
        r = lax.rem(lax.rem(i, n) + 1, n)
        qg = qs[r, pl.ds(pl.multiple_of(k * (nz * qn), nz * qn), nz * qn), :]
        wg = ws[r, pl.ds(k * nz, nz), :] * iscale
        sums = [[None] * nz, [None] * nz]
        nsb = sub // srows
        for sb in range(nsb):
            span = slice(sb * srows, (sb + 1) * srows)
            x = dot(keys_ref[span, :], qg, NT)
            grad = lg[span, :]
            side = sb * 2 // nsb
            for h in range(nz):
                xh = x[:, h * qn:(h + 1) * qn]
                gated = jnp.where(xh > 0.0, wg[h:h + 1, :] * grad, 0.0)
                pre[span, h * qn:(h + 1) * qn] = gated.astype(jnp.bfloat16)
                prod = jnp.maximum(xh, 0.0) * grad
                prod = jnp.sum(prod.reshape(srows // tail, tail, qn), axis=0)
                sums[side][h] = prod if sums[side][h] is None else sums[side][h] + prod
            gk_ref[span, :] += dot(pre[span, :], qg, NN)
        gq = dot(keys_t[...], pre[...], NN)
        for h in range(nz):
            for c in range(2):
                gbuf[i, c, h, 0:half, :] = gq[c * half:(c + 1) * half, h * qn:(h + 1) * qn]
                gbuf[i, c, h, half:half + tail, :] = sums[c][h]
        pair_copy(i).start()
        pl.when(i >= 1)(lambda: stage_pair(i - 1))
        at = lax.rem(i, n)
        pl.when((at == 2) & (i >= n))(lambda: stage_head(lax.div(i, n) - 1))
        pl.when((at == 0) & (i >= 2 * n))(lambda: stage_z(lax.div(i, n) - 2))
        pl.when((at == 2) & (i >= 2 * n))(lambda: stage_ag(lax.div(i, n) - 2))
        return carry

    lax.fori_loop(0, nstep, grad_step, 0)
    stage_pair(nstep - 1)
    head_done = max(nch - 1, 0)
    z_done = max(nch - 2, 0)
    for k in range(head_done, nch):
        stage_head(k)
    for k in range(z_done, nch):
        stage_z(k)
    for k in range(z_done, nch):
        stage_ag(k)

    for k in range(nch):
        for d in range(nz):
            fw_copy(k, d).wait_recv()
    for k in range(nch):
        res_ref[par, k, z] = fin[k]
        res_ref[1 - par, k, z] = res[1, k, nz - 1]
        for d in range(1, nz):
            src = lax.rem(z + nz - d, nz)
            res_ref[par, k, src] = res[0, k, d - 1]
            res_ref[1 - par, k, src] = res[1, k, d - 1]

    for i in range(nstep):
        pair_copy(i).wait_send()
        if (i % n + 1) % n:
            head_send(i, i // n, (i % n + 1) % n).wait_send()
    for k in range(nch):
        for d in range(1, nz):
            z_copy(k, d).wait_send()
            ag_copy(k, d).wait_send()
        for d in range(nz):
            fw_copy(k, d).wait_send()


def per_device(
    mla_queries, latent_cache, normalizers, query_positions, key_positions,
    index_queries, index_keys, index_weights,
):
    n = lax.axis_size("head")
    nc = lax.axis_size("ctx")
    nz = nc // 2
    mh, qn, lat = mla_queries.shape
    hl, _, width = index_queries.shape
    sub = index_keys.shape[0]
    nch = hl // nz
    nstep = nch * n
    rows = width // 2 + 8
    nblk = sub // min(sub, 512)
    own = lax.dynamic_slice_in_dim(
        key_positions, lax.axis_index("head") * sub, sub, 0)[:, None]
    f32 = jnp.float32
    dma = pltpu.SemaphoreType.DMA
    vm = pltpu.VMEM
    spec = pl.BlockSpec(memory_space=pltpu.VMEM)
    res, gk = pl.pallas_call(
        kernel,
        out_shape=(
            jax.ShapeDtypeStruct((2, nch, nz, rows, qn), f32),
            jax.ShapeDtypeStruct((sub, width), f32),
        ),
        in_specs=[spec] * 8,
        out_specs=(spec, spec),
        scratch_shapes=[
            vm((n, sub, qn), f32),
            vm((n - 1, sub, qn), f32),
            vm((n, hl * qn, width), jnp.bfloat16),
            vm((n, hl, qn), f32),
            vm((width, sub), jnp.bfloat16),
            vm((sub, qn), f32),
            vm((8, qn), f32),
            vm((n - 1, 8, qn), f32),
            vm((8, qn), f32),
            vm((nc - 1, 8, qn), f32),
            vm((sub, nz * qn), jnp.bfloat16),
            vm((nstep, 2, nz, rows, qn), f32),
            vm((nstep, nz, rows, qn), f32),
            vm((nstep, nz, rows, qn), f32),
            vm((nch, n - 1, nz, rows, qn), f32),
            vm((nch, nz, rows, qn), f32),
            vm((nch, nz - 1, rows, qn), f32),
            vm((nch, rows, qn), f32),
            vm((2, nch, nz, rows, qn), f32),
            vm((mh, qn), f32),
            dma(((n - 1) * nblk,)), dma(((n - 1) * nblk,)),
            dma((n - 1,)), dma((n - 1,)),
            dma((n - 1,)), dma((n - 1,)),
            dma((n - 1,)), dma((n - 1,)),
            dma((nc - 1,)), dma((nc - 1,)),
            dma((nstep,)), dma((nstep,)),
            dma((nstep,)), dma((nstep,)),
            dma((nch * nz,)), dma((nch * nz,)),
            dma((nch * nz,)), dma((nch * nz,)),
            dma((nch * nz,)), dma((nch * nz,)),
        ],
        compiler_params=pltpu.CompilerParams(
            collective_id=0, has_side_effects=True, vmem_limit_bytes=60 * 1024 * 1024),
    )(
        mla_queries.reshape(mh * qn, lat), latent_cache, normalizers,
        query_positions[None, :], own,
        index_queries.reshape(hl * qn, width), index_keys, index_weights,
    )
    half = width // 2
    body = res[:, :, :, :half, :].reshape(2, hl, half, qn)
    grad_queries = body.transpose(1, 3, 0, 2).reshape(hl, qn, width)
    scale = (n * hl * width) ** (-0.5)
    grad_weights = scale * jnp.sum(res[:, :, :, half:, :].reshape(2, hl, 8, qn), axis=(0, 2))
    return (grad_queries, grad_weights, gk)


def solution(mesh):
    placed = (
        P("head", None, None),
        P("ctx", None),
        P("head", None),
        P(),
        P("ctx"),
        P("head", None, None),
        P(("ctx", "head"), None),
        P("head", None),
    )
    return jax.shard_map(
        per_device,
        mesh=mesh,
        in_specs=placed,
        out_specs=(P("head", None, None), P("head", None), P(("ctx", "head"), None)),
        check_vma=False,
    )
```

time: 365 us -> 140 us (0.38)
  blocking collectives: 119 us -> 0 us
  Pallas kernels: 0 us -> 117 us
  matrix products: 90.2 us -> 0 us
  waiting for transfers between devices: 52.6 us -> 0 us
  other arithmetic: 40.7 us -> 1.59 us
  local copies, waits for them, and re-layouts: 38.5 us -> 20.5 us
  between operations: 14.6 us -> 0.67 us
  loops' own time: 5.59 us -> 0 us
    pallas_call x0 -> x1, Pallas kernels: none -> 117 us  [per_device(): pl.pallas_call(kernel, out_shape=(jax.ShapeDtypeStruct((2, nch, nz, rows,...]
    dot_general x11 -> x0, matrix products: 90.2 us -> none  [the longest x8 45.2 us: one_block(): jnp.dot(cache_rows, query_flat.T, preferred_element_type=jnp.float32)]
    psum x2 -> x0, blocking collectives: 59.2 us -> none  [the longest x1 41.1 us: per_device(): lax.psum((local_exp, local_target), ('head', 'ctx'))]
    pmax x1 -> x0, blocking collectives: 40.9 us -> none  [per_device(): row_max = lax.pmax(local_max, ('head', 'ctx'))]
    reduce_scatter x2 -> x0, waiting for transfers between devices: 37.5 us -> none  [the longest x1 37.5 us: per_device(): lax.psum_scatter(grad_queries_part, 'head', scatter_dimension=0, tiled=True)]
    reduce_sum x11 -> x1, other arithmetic: 38.1 us -> 0.99 us  [per_device(): jnp.sum(res[:, :, :, half:, :].reshape(2, hl, 8, qn), axis=(0, 2))]
    while x8 -> x0, local copies, waits for them, and re-layouts: 14.7 us -> none
    psum x1 -> x0, waiting for transfers between devices: 14.3 us -> none  [per_device(): grad_queries, grad_weights = lax.psum((head_queries, head_weights), 'ctx')]
  transfers between devices with their start and end apart: 4 -> 0, of which waited for: 2 -> 0; matrix products, arithmetic and copies ran while one was open for 41% -> 0% of each run, Pallas kernels for 0% -> 0%
where the time goes in v1:
time: 140 us
  Pallas kernels  117 us (84%)
  local copies, waits for them, and re-layouts  20.5 us (15%)
  other arithmetic  1.59 us (1%)
    pallas_call x1, Pallas kernels, per_device(): pl.pallas_call(kernel, out_shape=(jax.ShapeDtypeStruct((2, nch, nz, rows,...  117 us
    unnamed x6, local copies, waits for them, and re-layouts  17.4 us

profile of v1, /device:TPU:1, one launch (start us, length us, event | category | flops | bytes accessed | tf_op | source)
XLA Modules:
  0.0 139.9 jit_solution(841240691967450614)
XLA Ops:
  0.6 0.7 dynamic_slice.3
  1.3 1.0 copy.16.kpos_ref
  2.4 7.6 %copy.14 = bf16[32,128,576]{2,1,0:T(8,128)(2,1)} copy(bf16[32,128,576]{1,2,0:T(8,128)(2,1)} %param.8) | data formatting | bytes 9437184 | tf_op args[0]
  10.0 7.6 %copy.15.cache_ref = bf16[4096,576]{1,0:T(8,128)(2,1)} copy(bf16[4096,576]{0,1:T(8,128)(2,1)} %param.9) | data formatting | bytes 9437184 | tf_op args[1]
  17.6 117.1 %shard_map.103 = (f32[2,4,4,72,128]{4,3,2,1,0:T(8,128)}, f32[1024,128]{1,0:T(8,128)}) custom-call(bf16[4096,576]{1,0:T(8,128)(2,1)} %bitcast.9, bf16[4096,576]{1,0:T(8,128)(2,1)} %copy.15.cache_ref, f32[32,128]{1,0:T(8,128)} %norm_ref.1, s32[1,128]{1,0:T(1,128)} %bitcast.15, s32[1024,1]{1,0:T(8,128)} %copy.16.kpos_ref, bf16[2048,128]{1,0:T(8,128)(2,1)} %bitcast.12, ...), custom_call_target="tpu_custom_call" | custom-call | tf_op jit(solution)/shard_map/pallas_call | solution.py:343
  134.7 0.0 copy-start
  134.7 1.0 slice_reduce_fusion
  135.7 1.3 slice.6
  137.1 0.1 copy.17
  137.2 1.3 copy.18
  138.5 0.6 broadcast_multiply_fusion
  139.1 0.0 copy-done
  139.1 0.8 copy.20
Async XLA Ops:
  134.7 4.3 %copy-start = (f32[1024,128]{1,0:T(8,128)S(1)}, f32[1024,128]{1,0:T(8,128)}, u32[]{:S(2)}) copy-start(f32[1024,128]{1,0:T(8,128)} %get-tuple-element.15) | copy-start | bytes 1572868

commit v2 on v1

--- a/solution.py
+++ b/solution.py
@@ -22,11 +22,12 @@
 
 
 def kernel(
-    q_ref, cache_ref, norm_ref, qpos_ref, kpos_ref, iq_ref, keys_ref, iw_ref,
-    res_ref, gk_ref,
+    q_hbm, cache_hbm, norm_ref, qpos_ref, kpos_ref, iq_ref, keys_ref, iw_ref,
+    gq_ref, gw_ref, gk_ref,
+    q_ref, cache_ref, ct, kp,
     part, rp, qs, ws, keys_t, lg, stat, stat_h, stat2, stat_c, pre,
-    gbuf, pr, hs, hr, cs, zr, fin, res, nrm,
-    s_part, r_part, s_q, r_q, s_w, r_w, s_sh, r_sh, s_sc, r_sc,
+    gbuf, pr, hs, hr, cs, zr, fin, res, nrm, l_q, l_c,
+    s_part, r_part, s_q, r_q, s_qf, r_qf, s_w, r_w, s_sh, r_sh, s_sc, r_sc,
     s_pair, r_pair, s_head, r_head, s_z, r_z, s_ag, r_ag, s_fw, r_fw,
 ):
     n = lax.axis_size("head")
@@ -40,24 +41,51 @@
     sub, width = keys_ref.shape
     qn = qpos_ref.shape[1]
     hl = iw_ref.shape[0]
-    mh = q_ref.shape[0] // qn
+    mh = q_ref.shape[0]
     nch = hl // nz
     nstep = nch * n
     iscale = (n * hl * width) ** (-0.5)
 
+    wide = 2 if n % 2 == 0 else 1
+    deep = n // wide
+    hi = lax.div(me, deep)
+    lo = lax.rem(me, deep)
+
+    def ahead(rh, rl):
+        return lax.rem(hi + rh, wide) * deep + lax.rem(lo + rl, deep)
+
+    def block_owner(r):
+        return ahead(lax.div(r, deep), lax.rem(r, deep))
+
     def to_head(r):
         return {"head": lax.rem(me + r, n)}
 
-    def head_copy(src, dst, ss, rs, r):
+    def head_copy(src, dst, ss, rs, head):
         return pltpu.make_async_remote_copy(
             src_ref=src, dst_ref=dst, send_sem=ss, recv_sem=rs,
-            device_id=to_head(r), device_id_type=MESH)
+            device_id={"head": head}, device_id_type=MESH)
+
+    def hop(s, r):
+        rh, rl = r // deep, r % deep
+        first = rl > 0 if s == 0 else rh > 0
+        if s == 0:
+            return first, (ahead(0, rl) if first else ahead(rh, 0)), (rh * deep if first else 0)
+        return first, (ahead(rh, 0) if first else ahead(0, rl)), (rl if first else 0)
 
     def ctx_copy(src, dst, ss, rs, c):
         return pltpu.make_async_remote_copy(
             src_ref=src, dst_ref=dst, send_sem=ss, recv_sem=rs,
             device_id={"ctx": c}, device_id_type=MESH)
 
+    q_local = pltpu.make_async_copy(q_hbm, q_ref, l_q.at[0])
+    q_local.start()
+
+    def cache_copy(r):
+        cols = pl.ds(pl.multiple_of(block_owner(r) * sub, 128), sub)
+        return pltpu.make_async_copy(cache_hbm.at[:, cols], cache_ref.at[r], l_c.at[r])
+
+    for r in reversed(range(n)):
+        cache_copy(r).start()
     ws[0] = iw_ref[...].astype(jnp.float32)
     barrier = pltpu.get_barrier_semaphore()
     for r in range(1, n):
@@ -70,33 +98,79 @@
     nrm[...] = norm_ref[...] * log2e
     pl.semaphore_wait(barrier, n - 1 + nc - 1)
 
-    q_copies = []
+    qrows = hl * qn
+    mine = pl.ds(pl.multiple_of(par * (qrows // 2), qrows // 2), qrows // 2)
+
+    def q_copy(r):
+        rh, rl = r // deep, r % deep
+        return head_copy(
+            iq_ref.at[mine], qs.at[r, mine], s_q.at[r - 1], r_q.at[r - 1],
+            ahead(wide - rh, deep - rl))
+
+    def w_copy(r):
+        rh, rl = r // deep, r % deep
+        return head_copy(
+            ws.at[0], ws.at[r], s_w.at[r - 1], r_w.at[r - 1], ahead(wide - rh, deep - rl))
+
+    def q_forward(r):
+        return ctx_copy(
+            qs.at[r, mine], qs.at[r, mine], s_qf.at[r - 1], r_qf.at[r - 1], partner)
+
     for r in range(1, n):
-        q_copies.append(head_copy(iq_ref, qs.at[r], s_q.at[r - 1], r_q.at[r - 1], r))
-        q_copies.append(head_copy(ws.at[0], ws.at[r], s_w.at[r - 1], r_w.at[r - 1], r))
-    for copy in q_copies:
-        copy.start()
-
-    rows = min(sub, 512)
-    nblk = sub // rows
+        q_copy(r).start()
+        w_copy(r).start()
+
+    rows = sub // 2
     hg = 4
 
-    def part_copy(r, b):
-        span = pl.ds(pl.multiple_of(b * rows, rows), rows)
+    def part_copy(s, r):
+        _, head, _ = hop(s, r)
+        span = pl.ds(s * rows, rows)
+        at = s * n + r
         return head_copy(
-            part.at[r, span], rp.at[r - 1, span],
-            s_part.at[(r - 1) * nblk + b], r_part.at[(r - 1) * nblk + b], r)
+            part.at[r, span], rp.at[s, r - 1], s_part.at[at], r_part.at[at], head)
+
+    def part_gather(s, r):
+        span = slice(s * rows, (s + 1) * rows)
+        total = part[r, span, :]
+        for other in range(1, n):
+            if other != r and hop(s, other)[2] == r:
+                part_copy(s, other).wait_recv()
+                total = total + rp[s, other - 1]
+        part[r, span, :] = total
+
+    def after_block(s, r):
+        rh, rl = r // deep, r % deep
+        if r and hop(s, r)[0]:
+            part_copy(s, r).start()
+        if s == 1 and rh == 0 and rl > 0:
+            part_gather(1, rl)
+            part_copy(1, rl).start()
+            if rl == deep - 1:
+                for outer in range(1, wide):
+                    part_gather(0, outer * deep)
+                    part_copy(0, outer * deep).start()
+        if s == 0 and r == 0:
+            for other in range(1, n):
+                q_copy(other).wait_recv()
+                q_forward(other).start()
+
+    q_local.wait()
 
     def mla_step(i, carry):
-        r = lax.rem(lax.div(i, nblk) + 1, n)
-        b = lax.rem(i, nblk)
-        first = lax.rem(me + r, n) * sub + b * rows
-        cache = cache_ref[pl.ds(pl.multiple_of(first, rows), rows), :]
-        span = pl.ds(pl.multiple_of(b * rows, rows), rows)
+        r = n - 1 - lax.div(i, 2)
+        s = lax.rem(i, 2)
+        span = pl.ds(pl.multiple_of(s * rows, rows), rows)
+
+        @pl.when(s == 0)
+        def _():
+            cache_copy(r).wait()
+
+        ct[...] = cache_ref[r, :, span].T
 
         def group(g, acc_unused):
-            qg = q_ref[pl.ds(pl.multiple_of(g * (hg * qn), hg * qn), hg * qn), :]
-            x = dot(cache, qg, NT)
+            qg = jnp.concatenate([q_ref[g * hg + h] for h in range(hg)], axis=1)
+            x = dot(ct[...], qg, NN)
             total = None
             for h in range(hg):
                 e = jnp.exp2(
@@ -115,17 +189,16 @@
             return acc_unused
 
         lax.fori_loop(0, mh // hg, group, 0)
-
-        @pl.when(r > 0)
-        def _():
-            part_copy(r, b).start()
-
+        for j in range(2 * n):
+            pl.when(i == j)(functools.partial(after_block, j % 2, n - 1 - j // 2))
         return carry
 
-    lax.fori_loop(0, n * nblk, mla_step, 0)
-
-    for copy in q_copies:
-        copy.wait()
+    lax.fori_loop(0, 2 * n, mla_step, 0)
+
+    for r in range(1, n):
+        q_copy(r).wait_send()
+        w_copy(r).wait()
+        q_forward(r).wait()
     lg[...] = jnp.zeros_like(lg)
     srows = min(sub, 256)
     ih = nz
@@ -146,13 +219,13 @@
 
     lax.fori_loop(0, n * (hl // ih), logit_step, 0)
 
-    for r in range(1, n):
-        for b in range(nblk):
-            part_copy(r, b).wait()
-    visible = kpos_ref[...] <= qpos_ref[...]
+    for s in range(2):
+        part_gather(s, 0)
+    for block in range(sub // 128):
+        kp[block * 128:(block + 1) * 128, :] = jnp.broadcast_to(
+            kpos_ref[me, block:block + 1, :], (128, 128)).T
+    visible = kp[:, 0:qn] <= qpos_ref[...]
     probs = part[0]
-    for r in range(1, n):
-        probs = probs + rp[r - 1]
     probs = jnp.where(visible, probs, 0.0)
     part[0] = probs
     hidden = jnp.where(visible, lg[...] * iscale, masked_floor)
@@ -184,7 +257,8 @@
 
     stats = exchange(
         (local_max, local_sum, local_target), stat, stat_h, n,
-        lambda r: head_copy(stat, stat_h.at[r - 1], s_sh.at[r - 1], r_sh.at[r - 1], r))
+        lambda r: head_copy(
+            stat, stat_h.at[r - 1], s_sh.at[r - 1], r_sh.at[r - 1], lax.rem(me + r, n)))
     stats = exchange(
         stats, stat2, stat_c, nc,
         lambda r: ctx_copy(
@@ -200,8 +274,23 @@
     def pair_copy(i):
         return ctx_copy(gbuf.at[i, 1 - par], pr.at[i], s_pair.at[i], r_pair.at[i], partner)
 
-    def head_send(i, k, r):
-        return head_copy(hs.at[i], hr.at[k, r - 1], s_head.at[i], r_head.at[k * n + r], n - r)
+    hhalf = nz // 2
+
+    def head_send(k, s, r):
+        _, head, _ = hop(s, r)
+        span = pl.ds(s * hhalf, hhalf)
+        at = (k * 2 + s) * n + r
+        return head_copy(
+            hs.at[k, r, span], hr.at[k, r - 1, span], s_head.at[at], r_head.at[at], head)
+
+    def head_gather(k, s, r):
+        span = slice(s * hhalf, (s + 1) * hhalf)
+        total = hs[k, r, span]
+        for other in range(1, n):
+            if other != r and hop(s, other)[2] == r:
+                head_send(k, s, other).wait_recv()
+                total = total + hr[k, other - 1, span]
+        return total
 
     def z_copy(k, d):
         to = lax.rem(z + d, nz)
@@ -221,20 +310,26 @@
 
     def stage_pair(i):
         pair_copy(i).wait_recv()
-        hs[i] = gbuf[i, par] + pr[i]
         k = lax.div(i, n)
-        r = lax.rem(lax.rem(i, n) + 1, n)
-
-        @pl.when(r > 0)
-        def _():
-            head_send(i, k, r).start()
+        r = n - 1 - lax.rem(i, n)
+        hs[k, r] = gbuf[i, par] + pr[i]
+        for block in range(1, n):
+            def send(block=block):
+                for s in range(2):
+                    if hop(s, block)[0]:
+                        head_send(k, s, block).start()
+            pl.when(r == block)(send)
+
+    def stage_mid(k):
+        for s in range(2):
+            for r in range(1, n):
+                if not hop(s, r)[0]:
+                    hs[k, r, s * hhalf:(s + 1) * hhalf] = head_gather(k, s, r)
+                    head_send(k, s, r).start()
 
     def stage_head(k):
-        total = hs[k * n + n - 1]
-        for r in range(1, n):
-            head_send(k * n + r - 1, k, r).wait_recv()
-            total = total + hr[k, r - 1]
-        cs[k] = total
+        for s in range(2):
+            cs[k, s * hhalf:(s + 1) * hhalf] = head_gather(k, s, 0)
         for d in range(1, nz):
             z_copy(k, d).start()
 
@@ -255,7 +350,7 @@
 
     def grad_step(i, carry):
         k = lax.div(i, n)
-        r = lax.rem(lax.rem(i, n) + 1, n)
+        r = n - 1 - lax.rem(i, n)
         qg = qs[r, pl.ds(pl.multiple_of(k * (nz * qn), nz * qn), nz * qn), :]
         wg = ws[r, pl.ds(k * nz, nz), :] * iscale
         sums = [[None] * nz, [None] * nz]
@@ -281,6 +376,7 @@
         pair_copy(i).start()
         pl.when(i >= 1)(lambda: stage_pair(i - 1))
         at = lax.rem(i, n)
+        pl.when(at == n - 1)(lambda: stage_mid(lax.div(i, n)))
         pl.when((at == 2) & (i >= n))(lambda: stage_head(lax.div(i, n) - 1))
         pl.when((at == 0) & (i >= 2 * n))(lambda: stage_z(lax.div(i, n) - 2))
         pl.when((at == 2) & (i >= 2 * n))(lambda: stage_ag(lax.div(i, n) - 2))
@@ -301,23 +397,29 @@
         for d in range(nz):
             fw_copy(k, d).wait_recv()
     for k in range(nch):
-        res_ref[par, k, z] = fin[k]
-        res_ref[1 - par, k, z] = res[1, k, nz - 1]
-        for d in range(1, nz):
-            src = lax.rem(z + nz - d, nz)
-            res_ref[par, k, src] = res[0, k, d - 1]
-            res_ref[1 - par, k, src] = res[1, k, d - 1]
+        res[0, k, nz - 1] = fin[k]
+        for d in range(nz):
+            slot = nz - 1 if d == 0 else d - 1
+            head = k * nz + lax.rem(z + nz - d, nz)
+            low = res[par, k, slot]
+            high = res[1 - par, k, slot]
+            gq_ref[head] = jnp.concatenate([low[:half], high[:half]], axis=0).T
+            gw_ref[head] = iscale * jnp.sum(low[half:] + high[half:], axis=0, keepdims=True)
 
     for i in range(nstep):
         pair_copy(i).wait_send()
-        if (i % n + 1) % n:
-            head_send(i, i // n, (i % n + 1) % n).wait_send()
     for k in range(nch):
         for d in range(1, nz):
             z_copy(k, d).wait_send()
             ag_copy(k, d).wait_send()
         for d in range(nz):
             fw_copy(k, d).wait_send()
+        for s in range(2):
+            for r in range(1, n):
+                head_send(k, s, r).wait_send()
+    for s in range(2):
+        for r in range(1, n):
+            part_copy(s, r).wait_send()
 
 
 def per_device(
@@ -333,24 +435,27 @@
     nch = hl // nz
     nstep = nch * n
     rows = width // 2 + 8
-    nblk = sub // min(sub, 512)
-    own = lax.dynamic_slice_in_dim(
-        key_positions, lax.axis_index("head") * sub, sub, 0)[:, None]
     f32 = jnp.float32
     dma = pltpu.SemaphoreType.DMA
     vm = pltpu.VMEM
     spec = pl.BlockSpec(memory_space=pltpu.VMEM)
-    res, gk = pl.pallas_call(
+    hbm = pl.BlockSpec(memory_space=pl.ANY)
+    gq, gw, gk = pl.pallas_call(
         kernel,
         out_shape=(
-            jax.ShapeDtypeStruct((2, nch, nz, rows, qn), f32),
+            jax.ShapeDtypeStruct((hl, qn, width), f32),
+            jax.ShapeDtypeStruct((hl, 1, qn), f32),
             jax.ShapeDtypeStruct((sub, width), f32),
         ),
-        in_specs=[spec] * 8,
-        out_specs=(spec, spec),
+        in_specs=[hbm, hbm] + [spec] * 6,
+        out_specs=(spec, spec, spec),
         scratch_shapes=[
+            vm((mh, lat, qn), jnp.bfloat16),
+            vm((n, lat, sub), jnp.bfloat16),
+            vm((sub // 2, lat), jnp.bfloat16),
+            vm((sub, 128), jnp.int32),
             vm((n, sub, qn), f32),
-            vm((n - 1, sub, qn), f32),
+            vm((2, n - 1, sub // 2, qn), f32),
             vm((n, hl * qn, width), jnp.bfloat16),
             vm((n, hl, qn), f32),
             vm((width, sub), jnp.bfloat16),
@@ -362,20 +467,22 @@
             vm((sub, nz * qn), jnp.bfloat16),
             vm((nstep, 2, nz, rows, qn), f32),
             vm((nstep, nz, rows, qn), f32),
-            vm((nstep, nz, rows, qn), f32),
+            vm((nch, n, nz, rows, qn), f32),
             vm((nch, n - 1, nz, rows, qn), f32),
             vm((nch, nz, rows, qn), f32),
             vm((nch, nz - 1, rows, qn), f32),
             vm((nch, rows, qn), f32),
             vm((2, nch, nz, rows, qn), f32),
             vm((mh, qn), f32),
-            dma(((n - 1) * nblk,)), dma(((n - 1) * nblk,)),
+            dma((1,)), dma((n,)),
+            dma((2 * n,)), dma((2 * n,)),
+            dma((n - 1,)), dma((n - 1,)),
             dma((n - 1,)), dma((n - 1,)),
             dma((n - 1,)), dma((n - 1,)),
             dma((n - 1,)), dma((n - 1,)),
             dma((nc - 1,)), dma((nc - 1,)),
             dma((nstep,)), dma((nstep,)),
-            dma((nstep,)), dma((nstep,)),
+            dma((2 * nstep,)), dma((2 * nstep,)),
             dma((nch * nz,)), dma((nch * nz,)),
             dma((nch * nz,)), dma((nch * nz,)),
             dma((nch * nz,)), dma((nch * nz,)),
@@ -383,16 +490,11 @@
         compiler_params=pltpu.CompilerParams(
             collective_id=0, has_side_effects=True, vmem_limit_bytes=60 * 1024 * 1024),
     )(
-        mla_queries.reshape(mh * qn, lat), latent_cache, normalizers,
-        query_positions[None, :], own,
+        mla_queries.transpose(0, 2, 1), latent_cache.T, normalizers,
+        query_positions[None, :], key_positions.reshape(n, sub // 128, 128),
         index_queries.reshape(hl * qn, width), index_keys, index_weights,
     )
-    half = width // 2
-    body = res[:, :, :, :half, :].reshape(2, hl, half, qn)
-    grad_queries = body.transpose(1, 3, 0, 2).reshape(hl, qn, width)
-    scale = (n * hl * width) ** (-0.5)
-    grad_weights = scale * jnp.sum(res[:, :, :, half:, :].reshape(2, hl, 8, qn), axis=(0, 2))
-    return (grad_queries, grad_weights, gk)
+    return (gq, gw.reshape(hl, qn), gk)
 
 
 def solution(mesh):

time: 140 us -> 119 us (0.85)
  local copies, waits for them, and re-layouts: 20.5 us -> 5.46 us
  Pallas kernels: 117 us -> 113 us
  other arithmetic: 1.59 us -> 0 us
    unnamed x6 -> x3, local copies, waits for them, and re-layouts: 17.4 us -> 5.46 us
    pallas_call x1, Pallas kernels: 117 us -> 113 us  [per_device(): pl.pallas_call(kernel, out_shape=(jax.ShapeDtypeStruct((hl, qn, width), f...]
where the time goes in v2:
time: 119 us
  Pallas kernels  113 us (95%)
  local copies, waits for them, and re-layouts  5.46 us (5%)
    pallas_call x1, Pallas kernels, per_device(): pl.pallas_call(kernel, out_shape=(jax.ShapeDtypeStruct((hl, qn, width), f...  113 us
    unnamed x3, local copies, waits for them, and re-layouts  5.46 us

profile of v2, /device:TPU:1, one launch (start us, length us, event | category | flops | bytes accessed | tf_op | source)
XLA Modules:
  0.0 118.6 jit_solution(2476521324231728991)
XLA Ops:
  0.6 112.5 %shard_map.103 = (f32[16,128,128]{2,1,0:T(8,128)}, f32[16,1,128]{2,1,0:T(1,128)}, f32[1024,128]{1,0:T(8,128)}) custom-call(bf16[32,576,128]{2,1,0:T(8,128)(2,1)} %bitcast.6, bf16[576,4096]{1,0:T(8,128)(2,1)} %bitcast.7, f32[32,128]{1,0:T(8,128)} %norm_ref.1, s32[1,128]{1,0:T(1,128)} %bitcast.11, s32[4,8,128]{2,1,0:T(8,128)} %bitcast.9, ...), custom_call_target="tpu_custom_call" | custom-call | tf_op jit(solution)/shard_map/pallas_call | solution.py:443
  113.2 2.3 %copy.14 = f32[16,128,128]{2,1,0:T(8,128)} copy(f32[16,128,128]{2,1,0:T(8,128)} %get-tuple-element.12) | data formatting | bytes 2097152
  115.4 1.3 %copy.15 = f32[16,128]{1,0:T(8,128)} copy(f32[16,128]{1,0:T(8,128)} %bitcast.10) | data formatting | bytes 16384
  116.7 1.9 %copy.16 = f32[1024,128]{1,0:T(8,128)} copy(f32[1024,128]{1,0:T(8,128)} %get-tuple-element.14) | data formatting | bytes 1048576

commit v3 on v2

--- a/solution.py
+++ b/solution.py
@@ -122,6 +122,7 @@
 
     rows = sub // 2
     hg = 4
+    mrows = min(rows, 256)
 
     def part_copy(s, r):
         _, head, _ = hop(s, r)
@@ -168,27 +169,22 @@
 
         ct[...] = cache_ref[r, :, span].T
 
+        part[r, span, :] = jnp.zeros_like(part[r, span, :])
+
         def group(g, acc_unused):
             qg = jnp.concatenate([q_ref[g * hg + h] for h in range(hg)], axis=1)
-            x = dot(ct[...], qg, NN)
-            total = None
-            for h in range(hg):
-                e = jnp.exp2(
-                    x[:, h * qn:(h + 1) * qn] * (att_scale * log2e)
-                    - nrm[pl.ds(g * hg + h, 1), :])
-                total = e if total is None else total + e
-
-            @pl.when(g == 0)
-            def _():
-                part[r, span, :] = total
-
-            @pl.when(g > 0)
-            def _():
-                part[r, span, :] = part[r, span, :] + total
-
+            for sb in range(rows // mrows):
+                piece = pl.ds(pl.multiple_of(s * rows + sb * mrows, mrows), mrows)
+                x = dot(ct[sb * mrows:(sb + 1) * mrows, :], qg, NN)
+                total = part[r, piece, :]
+                for h in range(hg):
+                    total = total + jnp.exp2(
+                        x[:, h * qn:(h + 1) * qn] * (att_scale * log2e)
+                        - nrm[pl.ds(g * hg + h, 1), :])
+                part[r, piece, :] = total
             return acc_unused
 
-        lax.fori_loop(0, mh // hg, group, 0)
+        lax.fori_loop(0, mh // hg, group, 0, unroll=2)
         for j in range(2 * n):
             pl.when(i == j)(functools.partial(after_block, j % 2, n - 1 - j // 2))
         return carry

time: 119 us -> 112 us (0.941)
  Pallas kernels: 113 us -> 105 us
    pallas_call x1, Pallas kernels: 113 us -> 105 us  [per_device(): pl.pallas_call(kernel, out_shape=(jax.ShapeDtypeStruct((hl, qn, width), f...]
where the time goes in v3:
time: 112 us; the launch traced here: 111 us
  Pallas kernels  105 us (94%)
  local copies, waits for them, and re-layouts  5.46 us (5%)
    pallas_call x1, Pallas kernels, per_device(): pl.pallas_call(kernel, out_shape=(jax.ShapeDtypeStruct((hl, qn, width), f...  105 us
    unnamed x3, local copies, waits for them, and re-layouts  5.46 us

profile of v3, /device:TPU:1, one launch (start us, length us, event | category | flops | bytes accessed | tf_op | source)
XLA Modules:
  0.0 111.3 jit_solution(5795280229830636666)
XLA Ops:
  0.6 105.2 %shard_map.103 = (f32[16,128,128]{2,1,0:T(8,128)}, f32[16,1,128]{2,1,0:T(1,128)}, f32[1024,128]{1,0:T(8,128)}) custom-call(bf16[32,576,128]{2,1,0:T(8,128)(2,1)} %bitcast.6, bf16[576,4096]{1,0:T(8,128)(2,1)} %bitcast.7, f32[32,128]{1,0:T(8,128)} %norm_ref.1, s32[1,128]{1,0:T(1,128)} %bitcast.11, s32[4,8,128]{2,1,0:T(8,128)} %bitcast.9, ...), custom_call_target="tpu_custom_call" | custom-call | tf_op jit(solution)/shard_map/pallas_call | solution.py:439
  105.9 2.3 %copy.14 = f32[16,128,128]{2,1,0:T(8,128)} copy(f32[16,128,128]{2,1,0:T(8,128)} %get-tuple-element.12) | data formatting | bytes 2097152
  108.2 1.3 %copy.15 = f32[16,128]{1,0:T(8,128)} copy(f32[16,128]{1,0:T(8,128)} %bitcast.10) | data formatting | bytes 16384
  109.4 1.9 %copy.16 = f32[1024,128]{1,0:T(8,128)} copy(f32[1024,128]{1,0:T(8,128)} %get-tuple-element.14) | data formatting | bytes 1048576
